TPU v7x, 512 devices: a whole 4x8x8 slice. The times are simulated.
512 devices in a mesh: cuts: 32 (over x_lo, z, core), strip: 16 (over y, x_hi).
Axes of the slice: x: 4 (x_hi: 2, x_lo: 2; x = x_hi * 2 + x_lo), y: 8, z: 8, core: 2. Of those that a mesh axis runs over, the one named last changes fastest.
Arguments:
- field: float32 [128, 2, 512, 512], P('cuts', None, 'strip'), may hold values from -6 to 6
- phase: float32 [128, 16384], P('cuts', 'strip'), may hold values from -3.140625 to 3.140625
- energy: float32 [128, 16384], P('cuts', 'strip'), may hold values from -4 to 4
- row_bin: int32 [128, 16384], P('cuts', 'strip'), may hold values from 0 to 511, as said below
- col_bin: int32 [128, 16384], P('cuts', 'strip'), may hold values from 0 to 511
Outputs:
- field_out: float32 [128, 2, 512, 512], P('cuts', None, 'strip')
- phase_out: float32 [128, 16384], P('cuts', 'strip')
- energy_out: float32 [128, 16384], P('cuts', 'strip')
Inputs may be any that keep to these rules, and one draw needn't show every extreme that they name: `row_bin`: electron j of every slice sits in row strip j // 1024: its row lies in [(j // 1024) * 32, (j // 1024 + 1) * 32).
All inputs are finite; a program needn't handle non-finite values.
Results may differ from a plain program's by a relative error of at most 0.0014.
Values sent between devices are 32-bit elements; how exact they have to be, the bound alone decides.
A program may use at most 64 MiB of HBM per device.

v0:
```python
import functools
import math

import jax
import jax.numpy as jnp
import ml_dtypes
import numpy as np
from jax import lax
from jax.experimental import pallas as pl
from jax.experimental.pallas import tpu as pltpu
from jax.sharding import PartitionSpec as P

COUPLING = 0.5
DETUNING = 1.0
SOURCE_GAIN = 0.5
CHIRP_TOP = 60.0
MESH = pl.DeviceIdType.MESH
F32 = jnp.float32
BF16 = jnp.bfloat16


def axis_matrix(length):
    k = np.arange(length)
    q = np.where(k < length // 2, k, k - length) / (length // 2)
    response = np.fft.ifft(np.exp(-1j * CHIRP_TOP * q * q))
    matrix = response[(k[:, None] - k[None, :]) % length]
    both = np.concatenate([matrix.real, matrix.imag], axis=1).astype(np.float32)
    high = both.astype(ml_dtypes.bfloat16)
    low = (both - high.astype(np.float32)).astype(ml_dtypes.bfloat16)
    return high, low


def cos_sin(x):
    n = jnp.floor(x * (2.0 / math.pi) + 0.5)
    r = ((x - n * 1.5703125) - n * 4.837512969970703125e-4) - n * 7.549789948768648e-8
    z = r * r
    s = r + r * z * (-1.6666654611e-1 + z * (8.3321608736e-3 + z * -1.9515295891e-4))
    c = 1.0 - 0.5 * z + z * z * (
        4.166664568298827e-2 + z * (-1.388731625493765e-3 + z * 2.443315711809948e-5)
    )
    turn = n.astype(jnp.int32) & 3
    odd = (turn & 1) == 1
    cosine = jnp.where(odd, s, c)
    sine = jnp.where(odd, c, s)
    cosine = jnp.where((turn == 1) | (turn == 2), -cosine, cosine)
    sine = jnp.where(turn >= 2, -sine, sine)
    return cosine, sine


def split(x):
    high = x.astype(BF16)
    return high, (x - high.astype(F32)).astype(BF16)


def dot(a, b):
    return jnp.dot(a, b, preferred_element_type=F32)


def push(s, first_row, field_ref, phase_ref, energy_ref, row_ref, col_ref, phase_out, energy_out):
    rows = field_ref.shape[2]
    cols = field_ref.shape[3]
    count = phase_ref.shape[1]
    one = pl.ds(s, 1)
    field = field_ref[s].reshape(2 * rows, cols)
    phase = phase_ref[one, :]
    col_hot = jnp.where(
        lax.broadcasted_iota(jnp.int32, (cols, count), 0) == col_ref[one, :], 1.0, 0.0
    ).astype(BF16)
    row_hot = lax.broadcasted_iota(jnp.int32, (rows, count), 0) == row_ref[one, :] - first_row
    picked = dot(field.astype(BF16), col_hot)
    at_real = jnp.sum(jnp.where(row_hot, picked[:rows], 0.0), axis=0, keepdims=True)
    at_imag = jnp.sum(jnp.where(row_hot, picked[rows:], 0.0), axis=0, keepdims=True)
    cosine, sine = cos_sin(phase)
    energy_next = energy_ref[one, :] - COUPLING * (at_real * cosine - at_imag * sine)
    phase_next = phase + DETUNING * energy_next
    energy_out[one, :] = energy_next
    phase_out[one, :] = phase_next
    cosine, sine = cos_sin(phase_next)
    spread = jnp.concatenate(
        [jnp.where(row_hot, cosine, 0.0), jnp.where(row_hot, -sine, 0.0)], axis=0
    ).astype(BF16)
    deposit = lax.dot_general(spread, col_hot, (((1,), (1,)), ((), ())), preferred_element_type=F32)
    return field + SOURCE_GAIN * deposit


def turn_columns(driven, high_ref, low_ref):
    rows = driven.shape[0] // 2
    cols = driven.shape[1]
    high, low = split(driven)
    upper = dot(jnp.concatenate([high, low], axis=0), high_ref[...])
    total = upper[: 2 * rows] + upper[2 * rows :] + dot(high, low_ref[...])
    real = total[:rows, :cols] - total[rows:, cols:]
    imag = total[:rows, cols:] + total[rows:, :cols]
    return real, imag


def kernel(
    n_cuts,
    n_strip,
    field_ref,
    phase_ref,
    energy_ref,
    row_ref,
    col_ref,
    high_ref,
    low_ref,
    out_ref,
    phase_out,
    energy_out,
    turned,
    received,
    mixed,
    go_send,
    go_recv,
    back_send,
    back_recv,
):
    slices, _, rows, cols = field_ref.shape
    quarter = cols * slices // n_strip
    half = n_strip // 2
    groups = half // slices
    cut = lax.axis_index("cuts")
    me = lax.axis_index("strip")
    y, b = me // 2, me % 2
    my_slice = y % slices
    my_quarter = (y // slices) * 2 + b
    last = my_slice == slices - 1

    barrier = pltpu.get_barrier_semaphore()
    for d in range(1, n_strip):
        pl.semaphore_signal(
            barrier, inc=1, device_id={"cuts": cut, "strip": (me + d) % n_strip}, device_id_type=MESH
        )

    @pl.when(cut > 0)
    def _():
        for a in range(groups):
            for e in range(2):
                pl.semaphore_signal(
                    barrier,
                    inc=1,
                    device_id={"cuts": cut - 1, "strip": (a * slices + slices - 1) * 2 + e},
                    device_id_type=MESH,
                )

    sent = []
    for t in range(slices):
        s = (y + t) % slices
        driven = push(
            s, me * rows, field_ref, phase_ref, energy_ref, row_ref, col_ref, phase_out, energy_out
        )
        real, imag = turn_columns(driven, high_ref, low_ref)
        turned[s, 0] = real
        turned[s, 1] = imag
        if t == 0:
            peers = jnp.where(last & (cut < n_cuts - 1), 2 * n_strip - 1, n_strip - 1)
            pl.semaphore_wait(barrier, peers)

        for da in range(groups):
            for db in range(2):
                a = (y // slices + da) % groups
                e = (b + db) % 2
                target = (a * slices + s) * 2 + e
                lanes = pl.ds(pl.multiple_of((a * 2 + e) * quarter, quarter), quarter)
                source = turned.at[s, :, :, lanes]
                place = received.at[:, pl.ds(pl.multiple_of(me * rows, rows), rows), :]
                if t == 0 and da == 0 and db == 0:
                    copy = pltpu.make_async_copy(source, place, go_recv.at[me])
                else:
                    copy = pltpu.make_async_remote_copy(
                        src_ref=source,
                        dst_ref=place,
                        send_sem=go_send.at[t, da * 2 + db],
                        recv_sem=go_recv.at[me],
                        device_id={"cuts": cut, "strip": target},
                        device_id_type=MESH,
                    )
                copy.start()
                sent.append(copy)

    for i in range(n_strip):
        block = received.at[:, pl.ds(i * rows, rows), :]
        pltpu.make_async_copy(block, block, go_recv.at[i]).wait()
    for copy in sent[1:]:
        copy.wait_send()

    high, low = split(received[...])
    high = jnp.concatenate([high[0], high[1]], axis=1)
    low = jnp.concatenate([low[0], low[1]], axis=1)
    here = pl.ds(pl.multiple_of(my_quarter * quarter, quarter), quarter)
    steps = [half // 2]
    for d in range(half // 2 - 1, 0, -1):
        steps += [d, half - d]
    steps += [0]
    span = 2 * rows
    total_rows = high_ref.shape[0]
    for d in steps:
        to_y = (y + d) % half
        chunk = pl.ds(pl.multiple_of(to_y * span, span), span)
        factors = jnp.concatenate(
            [
                high_ref[chunk, :total_rows],
                high_ref[chunk, total_rows:],
                low_ref[chunk, :total_rows],
                low_ref[chunk, total_rows:],
            ],
            axis=0,
        )
        upper = dot(factors, high)
        total = upper[: 2 * span] + upper[2 * span :] + dot(factors[: 2 * span], low)
        mixed[0, chunk, :] = total[:span, :quarter] - total[span:, quarter:]
        mixed[1, chunk, :] = total[:span, quarter:] + total[span:, :quarter]
        for db in range(2):
            e = (b + db) % 2
            target = to_y * 2 + e
            source = mixed.at[:, pl.ds(pl.multiple_of(target * rows, rows), rows), :]

            @pl.when(jnp.logical_not(last))
            def _():
                place = out_ref.at[my_slice + 1, :, :, here]
                if d == 0 and db == 0:
                    pltpu.make_async_copy(source, place, back_recv.at[me]).start()
                else:
                    pltpu.make_async_remote_copy(
                        src_ref=source,
                        dst_ref=place,
                        send_sem=back_send.at[d * 2 + db],
                        recv_sem=back_recv.at[me],
                        device_id={"cuts": cut, "strip": target},
                        device_id_type=MESH,
                    ).start()

            @pl.when(last & (cut < n_cuts - 1))
            def _():
                pltpu.make_async_remote_copy(
                    src_ref=source,
                    dst_ref=out_ref.at[0, :, :, here],
                    send_sem=back_send.at[d * 2 + db],
                    recv_sem=back_recv.at[me],
                    device_id={"cuts": cut + 1, "strip": target},
                    device_id_type=MESH,
                ).start()

    @pl.when(cut == 0)
    def _():
        out_ref[0] = jnp.zeros(out_ref.shape[1:], F32)

    for i in range(n_strip):
        s = (i // 2) % slices
        lanes = pl.ds(((i // 2) // slices * 2 + i % 2) * quarter, quarter)
        block = out_ref.at[(s + 1) % slices, :, :, lanes]
        if s == slices - 1:

            @pl.when(cut > 0)
            def _():
                pltpu.make_async_copy(block, block, back_recv.at[i]).wait()
        else:
            pltpu.make_async_copy(block, block, back_recv.at[i]).wait()

    first = mixed.at[:, pl.ds(0, rows), :]
    for k in range(1, n_strip):

        @pl.when(jnp.logical_not(last) | (cut < n_cuts - 1))
        def _():
            pltpu.make_async_copy(first, first, back_send.at[k]).wait()

    @pl.when(last & (cut < n_cuts - 1))
    def _():
        pltpu.make_async_copy(first, first, back_send.at[0]).wait()


def shards(n_cuts, n_strip, field, phase, energy, row_bin, col_bin):
    slices, _, rows, cols = field.shape
    high, low = axis_matrix(cols)
    quarter = cols * slices // n_strip
    vmem = pl.BlockSpec(memory_space=pltpu.VMEM)
    dma = pltpu.SemaphoreType.DMA
    return pl.pallas_call(
        functools.partial(kernel, n_cuts, n_strip),
        out_shape=(
            jax.ShapeDtypeStruct(field.shape, F32),
            jax.ShapeDtypeStruct(phase.shape, F32),
            jax.ShapeDtypeStruct(energy.shape, F32),
        ),
        in_specs=[vmem] * 7,
        out_specs=(vmem,) * 3,
        scratch_shapes=[
            pltpu.VMEM(field.shape, F32),
            pltpu.VMEM((2, rows * n_strip, quarter), F32),
            pltpu.VMEM((2, rows * n_strip, quarter), F32),
            dma((slices, n_strip // slices)),
            dma((n_strip,)),
            dma((n_strip,)),
            dma((n_strip,)),
        ],
        compiler_params=pltpu.CompilerParams(collective_id=0, has_side_effects=True),
    )(field, phase, energy, row_bin, col_bin, jnp.asarray(high), jnp.asarray(low))


def solution(mesh):
    return jax.shard_map(
        functools.partial(shards, mesh.shape["cuts"], mesh.shape["strip"]),
        mesh=mesh,
        in_specs=(
            P("cuts", None, "strip", None),
            P("cuts", "strip"),
            P("cuts", "strip"),
            P("cuts", "strip"),
            P("cuts", "strip"),
        ),
        out_specs=(P("cuts", None, "strip", None), P("cuts", "strip"), P("cuts", "strip")),
        check_vma=False,
    )
```

profile of v0, /device:TPU:2, one launch (start us, length us, event | category | flops | bytes accessed | tf_op | source)
XLA Modules:
  0.0 51.8 jit_solution(9728435916906334567)
XLA Ops:
  0.6 47.9 %shard_map.94 = (f32[4,2,32,512]{3,2,1,0:T(8,128)}, f32[4,1024]{1,0:T(4,128)}, f32[4,1024]{1,0:T(4,128)}) custom-call(f32[4,2,32,512]{3,2,1,0:T(8,128)} %field_ref.1, f32[4,1024]{1,0:T(4,128)} %phase_ref.1, f32[4,1024]{1,0:T(4,128)} %energy_ref.1, s32[4,1024]{1,0:T(4,128)} %row_ref.1, s32[4,1024]{1,0:T(4,128)} %col_ref.1, ...), custom_call_target="tpu_custom_call" | custom-call | tf_op jit(solution)/shard_map/pallas_call | solution.py:278
  48.6 0.0 copy-start.1
  48.6 1.9 %copy.13 = f32[4,2,32,512]{3,2,1,0:T(8,128)} copy(f32[4,2,32,512]{3,2,1,0:T(8,128)} %get-tuple-element.6) | data formatting | bytes 1048576
  50.5 0.0 copy-done.1
  50.5 0.0 copy-start
  50.5 0.6 %copy.14 = f32[4,1024]{1,0:T(4,128)} copy(f32[4,1024]{1,0:T(4,128)S(1)} %copy-done.1) | data formatting | bytes 32768
  51.1 0.1 copy-done
  51.2 0.6 %copy.15 = f32[4,1024]{1,0:T(4,128)} copy(f32[4,1024]{1,0:T(4,128)S(1)} %copy-done) | data formatting | bytes 32768
Async XLA Ops:
  48.6 1.9 %copy-start.1 = (f32[4,1024]{1,0:T(4,128)S(1)}, f32[4,1024]{1,0:T(4,128)}, u32[]{:S(2)}) copy-start(f32[4,1024]{1,0:T(4,128)} %get-tuple-element.7) | copy-start | bytes 49156
  50.5 0.7 %copy-start = (f32[4,1024]{1,0:T(4,128)S(1)}, f32[4,1024]{1,0:T(4,128)}, u32[]{:S(2)}) copy-start(f32[4,1024]{1,0:T(4,128)} %get-tuple-element.8) | copy-start | bytes 49156
where the time goes:
time: 52 us; the launch traced here: 51.8 us
  Pallas kernels  47.9 us (92%)
  local copies, waits for them, and re-layouts  3.21 us (6%)
  between operations  0.65 us (1%)
    pallas_call x1, Pallas kernels, shards(): pl.pallas_call(functools.partial(kernel, n_cuts, n_strip), out_shape=(jax...  47.9 us
    unnamed x7, local copies, waits for them, and re-layouts  3.21 us

commit v1 on v0

--- a/solution.py
+++ b/solution.py
@@ -132,18 +132,13 @@
             barrier, inc=1, device_id={"cuts": cut, "strip": (me + d) % n_strip}, device_id_type=MESH
         )
 
-    @pl.when(cut > 0)
+    @pl.when(last & (cut > 0))
     def _():
-        for a in range(groups):
-            for e in range(2):
-                pl.semaphore_signal(
-                    barrier,
-                    inc=1,
-                    device_id={"cuts": cut - 1, "strip": (a * slices + slices - 1) * 2 + e},
-                    device_id_type=MESH,
-                )
-
-    sent = []
+        for i in range(n_strip):
+            pl.semaphore_signal(
+                barrier, inc=1, device_id={"cuts": cut - 1, "strip": i}, device_id_type=MESH
+            )
+
     for t in range(slices):
         s = (y + t) % slices
         driven = push(
@@ -153,7 +148,7 @@
         turned[s, 0] = real
         turned[s, 1] = imag
         if t == 0:
-            peers = jnp.where(last & (cut < n_cuts - 1), 2 * n_strip - 1, n_strip - 1)
+            peers = jnp.where(cut < n_cuts - 1, n_strip - 1 + n_strip // slices, n_strip - 1)
             pl.semaphore_wait(barrier, peers)
 
         for da in range(groups):
@@ -164,25 +159,38 @@
                 lanes = pl.ds(pl.multiple_of((a * 2 + e) * quarter, quarter), quarter)
                 source = turned.at[s, :, :, lanes]
                 place = received.at[:, pl.ds(pl.multiple_of(me * rows, rows), rows), :]
-                if t == 0 and da == 0 and db == 0:
-                    copy = pltpu.make_async_copy(source, place, go_recv.at[me])
-                else:
-                    copy = pltpu.make_async_remote_copy(
+                def send(to_cut):
+                    pltpu.make_async_remote_copy(
                         src_ref=source,
                         dst_ref=place,
                         send_sem=go_send.at[t, da * 2 + db],
                         recv_sem=go_recv.at[me],
-                        device_id={"cuts": cut, "strip": target},
+                        device_id={"cuts": to_cut, "strip": target},
                         device_id_type=MESH,
-                    )
-                copy.start()
-                sent.append(copy)
-
-    for i in range(n_strip):
-        block = received.at[:, pl.ds(i * rows, rows), :]
-        pltpu.make_async_copy(block, block, go_recv.at[i]).wait()
-    for copy in sent[1:]:
-        copy.wait_send()
+                    ).start()
+
+                @pl.when((s == slices - 1) & (cut < n_cuts - 1))
+                def _():
+                    send(cut + 1)
+
+                @pl.when(s < slices - 1)
+                def _():
+                    if t == 0 and da == 0 and db == 0:
+                        pltpu.make_async_copy(source, place, go_recv.at[me]).start()
+                    else:
+                        send(cut)
+
+    has_slice = jnp.logical_not(last) | (cut > 0)
+
+    @pl.when(has_slice)
+    def _():
+        for i in range(n_strip):
+            block = received.at[:, pl.ds(i * rows, rows), :]
+            pltpu.make_async_copy(block, block, go_recv.at[i]).wait()
+
+    @pl.when(jnp.logical_not(has_slice))
+    def _():
+        received[...] = jnp.zeros(received.shape, F32)
 
     high, low = split(received[...])
     high = jnp.concatenate([high[0], high[1]], axis=1)
@@ -215,58 +223,38 @@
             target = to_y * 2 + e
             source = mixed.at[:, pl.ds(pl.multiple_of(target * rows, rows), rows), :]
 
-            @pl.when(jnp.logical_not(last))
-            def _():
-                place = out_ref.at[my_slice + 1, :, :, here]
-                if d == 0 and db == 0:
-                    pltpu.make_async_copy(source, place, back_recv.at[me]).start()
-                else:
-                    pltpu.make_async_remote_copy(
-                        src_ref=source,
-                        dst_ref=place,
-                        send_sem=back_send.at[d * 2 + db],
-                        recv_sem=back_recv.at[me],
-                        device_id={"cuts": cut, "strip": target},
-                        device_id_type=MESH,
-                    ).start()
-
-            @pl.when(last & (cut < n_cuts - 1))
-            def _():
+            place = out_ref.at[(my_slice + 1) % slices, :, :, here]
+            if d == 0 and db == 0:
+                pltpu.make_async_copy(source, place, back_recv.at[me]).start()
+            else:
                 pltpu.make_async_remote_copy(
                     src_ref=source,
-                    dst_ref=out_ref.at[0, :, :, here],
+                    dst_ref=place,
                     send_sem=back_send.at[d * 2 + db],
                     recv_sem=back_recv.at[me],
-                    device_id={"cuts": cut + 1, "strip": target},
+                    device_id={"cuts": cut, "strip": target},
                     device_id_type=MESH,
                 ).start()
 
-    @pl.when(cut == 0)
-    def _():
-        out_ref[0] = jnp.zeros(out_ref.shape[1:], F32)
+    block = received.at[:, pl.ds(0, rows), :]
+    for t in range(slices):
+        s = (y + t) % slices
+        for k in range(n_strip // slices):
+            goes = (s == slices - 1) & (cut < n_cuts - 1)
+            if t > 0 or k > 0:
+                goes = goes | (s < slices - 1)
+
+            @pl.when(goes)
+            def _():
+                pltpu.make_async_copy(block, block, go_send.at[t, k]).wait()
 
     for i in range(n_strip):
-        s = (i // 2) % slices
         lanes = pl.ds(((i // 2) // slices * 2 + i % 2) * quarter, quarter)
-        block = out_ref.at[(s + 1) % slices, :, :, lanes]
-        if s == slices - 1:
-
-            @pl.when(cut > 0)
-            def _():
-                pltpu.make_async_copy(block, block, back_recv.at[i]).wait()
-        else:
-            pltpu.make_async_copy(block, block, back_recv.at[i]).wait()
-
-    first = mixed.at[:, pl.ds(0, rows), :]
+        block = out_ref.at[((i // 2) % slices + 1) % slices, :, :, lanes]
+        pltpu.make_async_copy(block, block, back_recv.at[i]).wait()
+    block = mixed.at[:, pl.ds(0, rows), :]
     for k in range(1, n_strip):
-
-        @pl.when(jnp.logical_not(last) | (cut < n_cuts - 1))
-        def _():
-            pltpu.make_async_copy(first, first, back_send.at[k]).wait()
-
-    @pl.when(last & (cut < n_cuts - 1))
-    def _():
-        pltpu.make_async_copy(first, first, back_send.at[0]).wait()
+        pltpu.make_async_copy(block, block, back_send.at[k]).wait()
 
 
 def shards(n_cuts, n_strip, field, phase, energy, row_bin, col_bin):

time: 52 us -> 47.5 us (0.913)
  the two profiles are of different devices: /device:TPU:2 before, /device:TPU:1 now
where the time goes in v1:
time: 47.5 us; the launch traced here: 47.2 us
  Pallas kernels  43.4 us (91%)
  local copies, waits for them, and re-layouts  3.21 us (7%)
  between operations  0.65 us (1%)
    pallas_call x1, Pallas kernels, shards(): pl.pallas_call(functools.partial(kernel, n_cuts, n_strip), out_shape=(jax...  43.4 us
    unnamed x7, local copies, waits for them, and re-layouts  3.21 us

profile of v1, /device:TPU:1, one launch (start us, length us, event | category | flops | bytes accessed | tf_op | source)
XLA Modules:
  0.0 47.2 jit_solution(11596955289439100348)
XLA Ops:
  0.6 43.4 %shard_map.94 = (f32[4,2,32,512]{3,2,1,0:T(8,128)}, f32[4,1024]{1,0:T(4,128)}, f32[4,1024]{1,0:T(4,128)}) custom-call(f32[4,2,32,512]{3,2,1,0:T(8,128)} %field_ref.1, f32[4,1024]{1,0:T(4,128)} %phase_ref.1, f32[4,1024]{1,0:T(4,128)} %energy_ref.1, s32[4,1024]{1,0:T(4,128)} %row_ref.1, s32[4,1024]{1,0:T(4,128)} %col_ref.1, ...), custom_call_target="tpu_custom_call" | custom-call | tf_op jit(solution)/shard_map/pallas_call | solution.py:266
  44.0 0.0 copy-start.1
  44.0 1.9 %copy.13 = f32[4,2,32,512]{3,2,1,0:T(8,128)} copy(f32[4,2,32,512]{3,2,1,0:T(8,128)} %get-tuple-element.6) | data formatting | bytes 1048576
  45.9 0.0 copy-done.1
  45.9 0.0 copy-start
  45.9 0.6 %copy.14 = f32[4,1024]{1,0:T(4,128)} copy(f32[4,1024]{1,0:T(4,128)S(1)} %copy-done.1) | data formatting | bytes 32768
  46.5 0.1 copy-done
  46.6 0.6 %copy.15 = f32[4,1024]{1,0:T(4,128)} copy(f32[4,1024]{1,0:T(4,128)S(1)} %copy-done) | data formatting | bytes 32768
Async XLA Ops:
  44.0 1.9 %copy-start.1 = (f32[4,1024]{1,0:T(4,128)S(1)}, f32[4,1024]{1,0:T(4,128)}, u32[]{:S(2)}) copy-start(f32[4,1024]{1,0:T(4,128)} %get-tuple-element.7) | copy-start | bytes 49156
  45.9 0.7 %copy-start = (f32[4,1024]{1,0:T(4,128)S(1)}, f32[4,1024]{1,0:T(4,128)}, u32[]{:S(2)}) copy-start(f32[4,1024]{1,0:T(4,128)} %get-tuple-element.8) | copy-start | bytes 49156

commit v2 on v1

--- a/solution.py
+++ b/solution.py
@@ -102,14 +102,17 @@
     energy_ref,
     row_ref,
     col_ref,
-    high_ref,
-    low_ref,
+    high_in,
+    low_in,
     out_ref,
     phase_out,
     energy_out,
+    high_ref,
+    low_ref,
     turned,
     received,
     mixed,
+    table_sem,
     go_send,
     go_recv,
     back_send,
@@ -119,6 +122,12 @@
     quarter = cols * slices // n_strip
     half = n_strip // 2
     groups = half // slices
+    tables = [
+        pltpu.make_async_copy(high_in, high_ref, table_sem.at[0]),
+        pltpu.make_async_copy(low_in, low_ref, table_sem.at[1]),
+    ]
+    for table in tables:
+        table.start()
     cut = lax.axis_index("cuts")
     me = lax.axis_index("strip")
     y, b = me // 2, me % 2
@@ -144,6 +153,9 @@
         driven = push(
             s, me * rows, field_ref, phase_ref, energy_ref, row_ref, col_ref, phase_out, energy_out
         )
+        if t == 0:
+            for table in tables:
+                table.wait()
         real, imag = turn_columns(driven, high_ref, low_ref)
         turned[s, 0] = real
         turned[s, 1] = imag
@@ -257,25 +269,41 @@
         pltpu.make_async_copy(block, block, back_send.at[k]).wait()
 
 
+def hand_out(field, phase, energy, field_out, phase_out, energy_out, sem):
+    copies = [
+        pltpu.make_async_copy(a, b, sem.at[i])
+        for i, (a, b) in enumerate(
+            ((field, field_out), (phase, phase_out), (energy, energy_out))
+        )
+    ]
+    for copy in copies:
+        copy.start()
+    for copy in copies:
+        copy.wait()
+
+
 def shards(n_cuts, n_strip, field, phase, energy, row_bin, col_bin):
     slices, _, rows, cols = field.shape
     high, low = axis_matrix(cols)
     quarter = cols * slices // n_strip
     vmem = pl.BlockSpec(memory_space=pltpu.VMEM)
     dma = pltpu.SemaphoreType.DMA
-    return pl.pallas_call(
+    moved = pl.pallas_call(
         functools.partial(kernel, n_cuts, n_strip),
         out_shape=(
-            jax.ShapeDtypeStruct(field.shape, F32),
-            jax.ShapeDtypeStruct(phase.shape, F32),
-            jax.ShapeDtypeStruct(energy.shape, F32),
+            pltpu.VMEM(field.shape, F32),
+            pltpu.VMEM(phase.shape, F32),
+            pltpu.VMEM(energy.shape, F32),
         ),
-        in_specs=[vmem] * 7,
+        in_specs=[vmem] * 5 + [pl.BlockSpec(memory_space=pl.ANY)] * 2,
         out_specs=(vmem,) * 3,
         scratch_shapes=[
+            pltpu.VMEM(high.shape, BF16),
+            pltpu.VMEM(low.shape, BF16),
             pltpu.VMEM(field.shape, F32),
             pltpu.VMEM((2, rows * n_strip, quarter), F32),
             pltpu.VMEM((2, rows * n_strip, quarter), F32),
+            dma((2,)),
             dma((slices, n_strip // slices)),
             dma((n_strip,)),
             dma((n_strip,)),
@@ -283,6 +311,13 @@
         ],
         compiler_params=pltpu.CompilerParams(collective_id=0, has_side_effects=True),
     )(field, phase, energy, row_bin, col_bin, jnp.asarray(high), jnp.asarray(low))
+    return pl.pallas_call(
+        hand_out,
+        out_shape=tuple(jax.ShapeDtypeStruct(x.shape, x.dtype) for x in moved),
+        in_specs=[pl.BlockSpec(memory_space=pltpu.VMEM)] * 3,
+        out_specs=(pl.BlockSpec(memory_space=pl.ANY),) * 3,
+        scratch_shapes=[dma((3,))],
+    )(*(pltpu.with_memory_space_constraint(x, pltpu.VMEM) for x in moved))
 
 
 def solution(mesh):

time: 47.5 us -> 43.4 us (0.914)
  the two profiles are of different devices: /device:TPU:1 before, /device:TPU:65 now
where the time goes in v2:
time: 43.4 us; the launch traced here: 43.2 us
  Pallas kernels  42.5 us (98%)
  between operations  0.64 us (1%)
    pallas_call x1, Pallas kernels, shards(): pl.pallas_call(functools.partial(kernel, n_cuts, n_strip), out_shape=(plt...  41.7 us

profile of v2, /device:TPU:65, one launch (start us, length us, event | category | flops | bytes accessed | tf_op | source)
XLA Modules:
  0.0 43.2 jit_solution(8181818226011796056)
XLA Ops:
  0.6 41.7 %shard_map.94 = (f32[4,2,32,512]{3,2,1,0:T(8,128)S(1)}, f32[4,1024]{1,0:T(4,128)S(1)}, f32[4,1024]{1,0:T(4,128)S(1)}) custom-call(f32[4,2,32,512]{3,2,1,0:T(8,128)} %field_ref.1, f32[4,1024]{1,0:T(4,128)} %phase_ref.1, f32[4,1024]{1,0:T(4,128)} %energy_ref.1, s32[4,1024]{1,0:T(4,128)} %row_ref.1, s32[4,1024]{1,0:T(4,128)} %col_ref.1, ...), custom_call_target="tpu_custom_call" | custom-call | tf_op jit(solution)/shard_map/pallas_call | solution.py:291
  42.4 0.8 %shard_map.95 = (f32[4,2,32,512]{3,2,1,0:T(8,128)}, f32[4,1024]{1,0:T(4,128)}, f32[4,1024]{1,0:T(4,128)}) custom-call(f32[4,2,32,512]{3,2,1,0:T(8,128)S(1)} %get-tuple-element.6.field, f32[4,1024]{1,0:T(4,128)S(1)} %get-tuple-element.7.phase, f32[4,1024]{1,0:T(4,128)S(1)} %get-tuple-element.8.energy), custom_call_target="tpu_custom_call" | custom-call | tf_op jit(solution)/shard_map/pallas_call | solution.py:314

commit v3 on v2

--- a/solution.py
+++ b/solution.py
@@ -97,37 +97,39 @@
 def kernel(
     n_cuts,
     n_strip,
+    field_in,
+    phase_in,
+    energy_in,
+    row_in,
+    col_in,
+    high_in,
+    low_in,
+    out_ref,
+    phase_out,
+    energy_out,
     field_ref,
     phase_ref,
     energy_ref,
     row_ref,
     col_ref,
-    high_in,
-    low_in,
-    out_ref,
-    phase_out,
-    energy_out,
     high_ref,
     low_ref,
     turned,
     received,
+    upper_half,
+    lower_half,
     mixed,
-    table_sem,
+    load_sem,
+    field_sem,
     go_send,
     go_recv,
     back_send,
     back_recv,
 ):
-    slices, _, rows, cols = field_ref.shape
+    slices, _, rows, cols = field_in.shape
     quarter = cols * slices // n_strip
     half = n_strip // 2
     groups = half // slices
-    tables = [
-        pltpu.make_async_copy(high_in, high_ref, table_sem.at[0]),
-        pltpu.make_async_copy(low_in, low_ref, table_sem.at[1]),
-    ]
-    for table in tables:
-        table.start()
     cut = lax.axis_index("cuts")
     me = lax.axis_index("strip")
     y, b = me // 2, me % 2
@@ -148,8 +150,36 @@
                 barrier, inc=1, device_id={"cuts": cut - 1, "strip": i}, device_id_type=MESH
             )
 
+    electrons = [
+        pltpu.make_async_copy(a, b, load_sem.at[i])
+        for i, (a, b) in enumerate(
+            (
+                (phase_in, phase_ref),
+                (energy_in, energy_ref),
+                (row_in, row_ref),
+                (col_in, col_ref),
+            )
+        )
+    ]
+    fields = [
+        pltpu.make_async_copy(
+            field_in.at[(y + t) % slices], field_ref.at[(y + t) % slices], field_sem.at[t]
+        )
+        for t in range(slices)
+    ]
+    tables = [
+        pltpu.make_async_copy(high_in, high_ref, load_sem.at[4]),
+        pltpu.make_async_copy(low_in, low_ref, load_sem.at[5]),
+    ]
+    for load in [*electrons, *fields[:1], *tables, *fields[1:]]:
+        load.start()
+
     for t in range(slices):
         s = (y + t) % slices
+        if t == 0:
+            for load in electrons:
+                load.wait()
+        fields[t].wait()
         driven = push(
             s, me * rows, field_ref, phase_ref, energy_ref, row_ref, col_ref, phase_out, energy_out
         )
@@ -196,17 +226,28 @@
 
     @pl.when(has_slice)
     def _():
-        for i in range(n_strip):
-            block = received.at[:, pl.ds(i * rows, rows), :]
-            pltpu.make_async_copy(block, block, go_recv.at[i]).wait()
+        near = [0]
+        for d in range(1, half // 2):
+            near += [d, half - d]
+        for d in near + [half // 2]:
+            for db in range(2):
+                i = (y + d) % half * 2 + (b + db) % 2
+                block = pl.ds(pl.multiple_of(i * rows, rows), rows)
+                place = received.at[:, block, :]
+                pltpu.make_async_copy(place, place, go_recv.at[i]).wait()
+                for part in range(2):
+                    lanes = pl.ds(part * quarter, quarter)
+                    upper, lower = split(received[part, block, :])
+                    upper_half[block, lanes] = upper
+                    lower_half[block, lanes] = lower
 
     @pl.when(jnp.logical_not(has_slice))
     def _():
-        received[...] = jnp.zeros(received.shape, F32)
-
-    high, low = split(received[...])
-    high = jnp.concatenate([high[0], high[1]], axis=1)
-    low = jnp.concatenate([low[0], low[1]], axis=1)
+        upper_half[...] = jnp.zeros(upper_half.shape, BF16)
+        lower_half[...] = jnp.zeros(lower_half.shape, BF16)
+
+    high = upper_half[...]
+    low = lower_half[...]
     here = pl.ds(pl.multiple_of(my_quarter * quarter, quarter), quarter)
     steps = [half // 2]
     for d in range(half // 2 - 1, 0, -1):
@@ -295,15 +336,19 @@
             pltpu.VMEM(phase.shape, F32),
             pltpu.VMEM(energy.shape, F32),
         ),
-        in_specs=[vmem] * 5 + [pl.BlockSpec(memory_space=pl.ANY)] * 2,
+        in_specs=[pl.BlockSpec(memory_space=pl.ANY)] * 7,
         out_specs=(vmem,) * 3,
         scratch_shapes=[
+            *(pltpu.VMEM(x.shape, x.dtype) for x in (field, phase, energy, row_bin, col_bin)),
             pltpu.VMEM(high.shape, BF16),
             pltpu.VMEM(low.shape, BF16),
             pltpu.VMEM(field.shape, F32),
             pltpu.VMEM((2, rows * n_strip, quarter), F32),
+            pltpu.VMEM((rows * n_strip, 2 * quarter), BF16),
+            pltpu.VMEM((rows * n_strip, 2 * quarter), BF16),
             pltpu.VMEM((2, rows * n_strip, quarter), F32),
-            dma((2,)),
+            dma((6,)),
+            dma((slices,)),
             dma((slices, n_strip // slices)),
             dma((n_strip,)),
             dma((n_strip,)),

time: 43.4 us -> 42.6 us (0.982)
  Pallas kernels: 42.5 us -> 41.7 us
    pallas_call x1, Pallas kernels: 41.7 us -> 40.9 us  [shards(): pl.pallas_call(functools.partial(kernel, n_cuts, n_strip), out_shape=(plt...]
where the time goes in v3:
time: 42.6 us; the launch traced here: 42.4 us
  Pallas kernels  41.7 us (98%)
  between operations  0.64 us (2%)
    pallas_call x1, Pallas kernels, shards(): pl.pallas_call(functools.partial(kernel, n_cuts, n_strip), out_shape=(plt...  40.9 us

profile of v3, /device:TPU:65, one launch (start us, length us, event | category | flops | bytes accessed | tf_op | source)
XLA Modules:
  0.0 42.4 jit_solution(11638905634175052851)
XLA Ops:
  0.6 40.9 %shard_map.94 = (f32[4,2,32,512]{3,2,1,0:T(8,128)S(1)}, f32[4,1024]{1,0:T(4,128)S(1)}, f32[4,1024]{1,0:T(4,128)S(1)}) custom-call(f32[4,2,32,512]{3,2,1,0:T(8,128)} %field_in.1, f32[4,1024]{1,0:T(4,128)} %phase_in.1, f32[4,1024]{1,0:T(4,128)} %energy_in.1, s32[4,1024]{1,0:T(4,128)} %row_in.1, s32[4,1024]{1,0:T(4,128)} %col_in.1, ...), custom_call_target="tpu_custom_call" | custom-call | tf_op jit(solution)/shard_map/pallas_call | solution.py:332
  41.6 0.8 %shard_map.95 = (f32[4,2,32,512]{3,2,1,0:T(8,128)}, f32[4,1024]{1,0:T(4,128)}, f32[4,1024]{1,0:T(4,128)}) custom-call(f32[4,2,32,512]{3,2,1,0:T(8,128)S(1)} %get-tuple-element.6.field, f32[4,1024]{1,0:T(4,128)S(1)} %get-tuple-element.7.phase, f32[4,1024]{1,0:T(4,128)S(1)} %get-tuple-element.8.energy), custom_call_target="tpu_custom_call" | custom-call | tf_op jit(solution)/shard_map/pallas_call | solution.py:359

commit v4 on v3

--- a/solution.py
+++ b/solution.py
@@ -116,9 +116,8 @@
     low_ref,
     turned,
     received,
-    upper_half,
-    lower_half,
     mixed,
+    landed,
     load_sem,
     field_sem,
     go_send,
@@ -174,6 +173,46 @@
     for load in [*electrons, *fields[:1], *tables, *fields[1:]]:
         load.start()
 
+    def send_slice(t, h):
+        s = (y + t) % slices
+        for da in range(groups):
+            for db in range(2):
+                a = (y // slices + da) % groups
+                e = (b + db) % 2
+                target = (a * slices + s) * 2 + e
+                lanes = pl.ds(pl.multiple_of((a * 2 + e) * quarter, quarter), quarter)
+                source = turned.at[s, h, :, lanes]
+                place = received.at[h, pl.ds(pl.multiple_of(me * rows, rows), rows), :]
+
+                def send(to_cut):
+                    pltpu.make_async_remote_copy(
+                        src_ref=source,
+                        dst_ref=place,
+                        send_sem=go_send.at[h, t, da * 2 + db],
+                        recv_sem=go_recv.at[h, me],
+                        device_id={"cuts": to_cut, "strip": target},
+                        device_id_type=MESH,
+                    ).start()
+
+                @pl.when((s == slices - 1) & (cut < n_cuts - 1))
+                def _():
+                    send(cut + 1)
+
+                @pl.when(s < slices - 1)
+                def _():
+                    if t == 0 and da == 0 and db == 0:
+                        pltpu.make_async_copy(source, place, go_recv.at[h, me]).start()
+                    else:
+                        send(cut)
+
+    left = lax.broadcasted_iota(jnp.int32, (rows, quarter), 1) < quarter // 2
+
+    def pick(x, z):
+        return jnp.where(left, x, z)
+
+    def turn(x):
+        return pltpu.roll(x, quarter // 2, 1)
+
     for t in range(slices):
         s = (y + t) % slices
         if t == 0:
@@ -187,109 +226,80 @@
             for table in tables:
                 table.wait()
         real, imag = turn_columns(driven, high_ref, low_ref)
-        turned[s, 0] = real
-        turned[s, 1] = imag
+        for q in range(cols // quarter):
+            lanes = pl.ds(q * quarter, quarter)
+            re = real[:, q * quarter : (q + 1) * quarter]
+            im = imag[:, q * quarter : (q + 1) * quarter]
+            turned[s, 0, :, lanes] = pick(re, turn(im))
+            turned[s, 1, :, lanes] = pick(turn(re), im)
         if t == 0:
             peers = jnp.where(cut < n_cuts - 1, n_strip - 1 + n_strip // slices, n_strip - 1)
             pl.semaphore_wait(barrier, peers)
 
-        for da in range(groups):
-            for db in range(2):
-                a = (y // slices + da) % groups
-                e = (b + db) % 2
-                target = (a * slices + s) * 2 + e
-                lanes = pl.ds(pl.multiple_of((a * 2 + e) * quarter, quarter), quarter)
-                source = turned.at[s, :, :, lanes]
-                place = received.at[:, pl.ds(pl.multiple_of(me * rows, rows), rows), :]
-                def send(to_cut):
-                    pltpu.make_async_remote_copy(
-                        src_ref=source,
-                        dst_ref=place,
-                        send_sem=go_send.at[t, da * 2 + db],
-                        recv_sem=go_recv.at[me],
-                        device_id={"cuts": to_cut, "strip": target},
-                        device_id_type=MESH,
-                    ).start()
-
-                @pl.when((s == slices - 1) & (cut < n_cuts - 1))
-                def _():
-                    send(cut + 1)
-
-                @pl.when(s < slices - 1)
-                def _():
-                    if t == 0 and da == 0 and db == 0:
-                        pltpu.make_async_copy(source, place, go_recv.at[me]).start()
-                    else:
-                        send(cut)
+        send_slice(t, 0)
+    for t in range(slices):
+        send_slice(t, 1)
 
     has_slice = jnp.logical_not(last) | (cut > 0)
 
-    @pl.when(has_slice)
-    def _():
-        near = [0]
-        for d in range(1, half // 2):
-            near += [d, half - d]
-        for d in near + [half // 2]:
-            for db in range(2):
-                i = (y + d) % half * 2 + (b + db) % 2
-                block = pl.ds(pl.multiple_of(i * rows, rows), rows)
-                place = received.at[:, block, :]
-                pltpu.make_async_copy(place, place, go_recv.at[i]).wait()
-                for part in range(2):
-                    lanes = pl.ds(part * quarter, quarter)
-                    upper, lower = split(received[part, block, :])
-                    upper_half[block, lanes] = upper
-                    lower_half[block, lanes] = lower
-
-    @pl.when(jnp.logical_not(has_slice))
-    def _():
-        upper_half[...] = jnp.zeros(upper_half.shape, BF16)
-        lower_half[...] = jnp.zeros(lower_half.shape, BF16)
-
-    high = upper_half[...]
-    low = lower_half[...]
-    here = pl.ds(pl.multiple_of(my_quarter * quarter, quarter), quarter)
     steps = [half // 2]
     for d in range(half // 2 - 1, 0, -1):
         steps += [d, half - d]
     steps += [0]
     span = 2 * rows
     total_rows = high_ref.shape[0]
-    for d in steps:
-        to_y = (y + d) % half
-        chunk = pl.ds(pl.multiple_of(to_y * span, span), span)
-        factors = jnp.concatenate(
-            [
-                high_ref[chunk, :total_rows],
-                high_ref[chunk, total_rows:],
-                low_ref[chunk, :total_rows],
-                low_ref[chunk, total_rows:],
-            ],
-            axis=0,
-        )
-        upper = dot(factors, high)
-        total = upper[: 2 * span] + upper[2 * span :] + dot(factors[: 2 * span], low)
-        mixed[0, chunk, :] = total[:span, :quarter] - total[span:, quarter:]
-        mixed[1, chunk, :] = total[:span, quarter:] + total[span:, :quarter]
-        for db in range(2):
-            e = (b + db) % 2
-            target = to_y * 2 + e
-            source = mixed.at[:, pl.ds(pl.multiple_of(target * rows, rows), rows), :]
-
-            place = out_ref.at[(my_slice + 1) % slices, :, :, here]
-            if d == 0 and db == 0:
-                pltpu.make_async_copy(source, place, back_recv.at[me]).start()
-            else:
-                pltpu.make_async_remote_copy(
-                    src_ref=source,
-                    dst_ref=place,
-                    send_sem=back_send.at[d * 2 + db],
-                    recv_sem=back_recv.at[me],
-                    device_id={"cuts": cut, "strip": target},
-                    device_id_type=MESH,
-                ).start()
-
-    block = received.at[:, pl.ds(0, rows), :]
+    first_half = lax.broadcasted_iota(jnp.int32, (span, quarter), 1) < quarter // 2
+
+    for h in range(2):
+
+        @pl.when(has_slice)
+        def _():
+            for i in range(n_strip):
+                block = received.at[h, pl.ds(i * rows, rows), :]
+                pltpu.make_async_copy(block, block, go_recv.at[h, i]).wait()
+
+        @pl.when(jnp.logical_not(has_slice))
+        def _():
+            received[h] = jnp.zeros((total_rows, quarter), F32)
+
+        both = jnp.concatenate(split(received[h]), axis=1)
+        for d in steps:
+            to_y = (y + d) % half
+            chunk = pl.ds(pl.multiple_of(to_y * span, span), span)
+            factors = jnp.concatenate(
+                [
+                    high_ref[chunk, :total_rows],
+                    high_ref[chunk, total_rows:],
+                    low_ref[chunk, :total_rows],
+                    low_ref[chunk, total_rows:],
+                ],
+                axis=0,
+            )
+            upper = dot(factors, both)
+            total = (
+                upper[: 2 * span, :quarter]
+                + upper[2 * span :, :quarter]
+                + upper[: 2 * span, quarter:]
+            )
+            cross = turn(total[span:])
+            mixed[h, chunk, :] = total[:span] + jnp.where(first_half, -cross, cross)
+            for db in range(2):
+                target = to_y * 2 + (b + db) % 2
+                source = mixed.at[h, pl.ds(pl.multiple_of(target * rows, rows), rows), :]
+                place = landed.at[(my_slice + 1) % slices, my_quarter, h]
+                if d == 0 and db == 0:
+                    pltpu.make_async_copy(source, place, back_recv.at[h, me]).start()
+                else:
+                    pltpu.make_async_remote_copy(
+                        src_ref=source,
+                        dst_ref=place,
+                        send_sem=back_send.at[h, d * 2 + db],
+                        recv_sem=back_recv.at[h, me],
+                        device_id={"cuts": cut, "strip": target},
+                        device_id_type=MESH,
+                    ).start()
+
+    block = received.at[0, pl.ds(0, rows), :]
     for t in range(slices):
         s = (y + t) % slices
         for k in range(n_strip // slices):
@@ -299,15 +309,21 @@
 
             @pl.when(goes)
             def _():
-                pltpu.make_async_copy(block, block, go_send.at[t, k]).wait()
+                for h in range(2):
+                    pltpu.make_async_copy(block, block, go_send.at[h, t, k]).wait()
 
     for i in range(n_strip):
-        lanes = pl.ds(((i // 2) // slices * 2 + i % 2) * quarter, quarter)
-        block = out_ref.at[((i // 2) % slices + 1) % slices, :, :, lanes]
-        pltpu.make_async_copy(block, block, back_recv.at[i]).wait()
-    block = mixed.at[:, pl.ds(0, rows), :]
+        slot, q = ((i // 2) % slices + 1) % slices, (i // 2) // slices * 2 + i % 2
+        lanes = pl.ds(q * quarter, quarter)
+        for h in range(2):
+            place = landed.at[slot, q, h]
+            pltpu.make_async_copy(place, place, back_recv.at[h, i]).wait()
+        one, two = landed[slot, q, 0], landed[slot, q, 1]
+        out_ref[slot, 0, :, lanes] = pick(one, turn(two))
+        out_ref[slot, 1, :, lanes] = pick(turn(one), two)
     for k in range(1, n_strip):
-        pltpu.make_async_copy(block, block, back_send.at[k]).wait()
+        for h in range(2):
+            pltpu.make_async_copy(block, block, back_send.at[h, k]).wait()
 
 
 def hand_out(field, phase, energy, field_out, phase_out, energy_out, sem):
@@ -344,15 +360,14 @@
             pltpu.VMEM(low.shape, BF16),
             pltpu.VMEM(field.shape, F32),
             pltpu.VMEM((2, rows * n_strip, quarter), F32),
-            pltpu.VMEM((rows * n_strip, 2 * quarter), BF16),
-            pltpu.VMEM((rows * n_strip, 2 * quarter), BF16),
             pltpu.VMEM((2, rows * n_strip, quarter), F32),
+            pltpu.VMEM((slices, cols // quarter, 2, rows, quarter), F32),
             dma((6,)),
             dma((slices,)),
-            dma((slices, n_strip // slices)),
-            dma((n_strip,)),
-            dma((n_strip,)),
-            dma((n_strip,)),
+            dma((2, slices, n_strip // slices)),
+            dma((2, n_strip)),
+            dma((2, n_strip)),
+            dma((2, n_strip)),
         ],
         compiler_params=pltpu.CompilerParams(collective_id=0, has_side_effects=True),
     )(field, phase, energy, row_bin, col_bin, jnp.asarray(high), jnp.asarray(low))

time: 42.6 us -> 41.3 us (0.969)
  the two profiles are of different devices: /device:TPU:65 before, /device:TPU:2 now
where the time goes in v4:
time: 41.3 us; the launch traced here: 41.1 us
  Pallas kernels  40.5 us (98%)
  between operations  0.64 us (2%)
    pallas_call x1, Pallas kernels, shards(): pl.pallas_call(functools.partial(kernel, n_cuts, n_strip), out_shape=(plt...  39.6 us

profile of v4, /device:TPU:2, one launch (start us, length us, event | category | flops | bytes accessed | tf_op | source)
XLA Modules:
  0.0 41.1 jit_solution(16062096149245827386)
XLA Ops:
  0.6 39.6 %shard_map.94 = (f32[4,2,32,512]{3,2,1,0:T(8,128)S(1)}, f32[4,1024]{1,0:T(4,128)S(1)}, f32[4,1024]{1,0:T(4,128)S(1)}) custom-call(f32[4,2,32,512]{3,2,1,0:T(8,128)} %field_in.1, f32[4,1024]{1,0:T(4,128)} %phase_in.1, f32[4,1024]{1,0:T(4,128)} %energy_in.1, s32[4,1024]{1,0:T(4,128)} %row_in.1, s32[4,1024]{1,0:T(4,128)} %col_in.1, ...), custom_call_target="tpu_custom_call" | custom-call | tf_op jit(solution)/shard_map/pallas_call | solution.py:348
  40.3 0.8 %shard_map.95 = (f32[4,2,32,512]{3,2,1,0:T(8,128)}, f32[4,1024]{1,0:T(4,128)}, f32[4,1024]{1,0:T(4,128)}) custom-call(f32[4,2,32,512]{3,2,1,0:T(8,128)S(1)} %get-tuple-element.6.field, f32[4,1024]{1,0:T(4,128)S(1)} %get-tuple-element.7.phase, f32[4,1024]{1,0:T(4,128)S(1)} %get-tuple-element.8.energy), custom_call_target="tpu_custom_call" | custom-call | tf_op jit(solution)/shard_map/pallas_call | solution.py:374

commit v5 on v4

--- a/solution.py
+++ b/solution.py
@@ -312,9 +312,11 @@
                 for h in range(2):
                     pltpu.make_async_copy(block, block, go_send.at[h, t, k]).wait()
 
-    for i in range(n_strip):
-        slot, q = ((i // 2) % slices + 1) % slices, (i // 2) // slices * 2 + i % 2
-        lanes = pl.ds(q * quarter, quarter)
+    for d, db in [(d, db) for d in steps for db in range(2)]:
+        from_y, e = (y - d + half) % half, (b + db) % 2
+        i = from_y * 2 + e
+        slot, q = (from_y % slices + 1) % slices, from_y // slices * 2 + e
+        lanes = pl.ds(pl.multiple_of(q * quarter, quarter), quarter)
         for h in range(2):
             place = landed.at[slot, q, h]
             pltpu.make_async_copy(place, place, back_recv.at[h, i]).wait()
@@ -330,7 +332,11 @@
     copies = [
         pltpu.make_async_copy(a, b, sem.at[i])
         for i, (a, b) in enumerate(
-            ((field, field_out), (phase, phase_out), (energy, energy_out))
+            (
+                *((field.at[s], field_out.at[s]) for s in range(field.shape[0])),
+                (phase, phase_out),
+                (energy, energy_out),
+            )
         )
     ]
     for copy in copies:
@@ -376,7 +382,7 @@
         out_shape=tuple(jax.ShapeDtypeStruct(x.shape, x.dtype) for x in moved),
         in_specs=[pl.BlockSpec(memory_space=pltpu.VMEM)] * 3,
         out_specs=(pl.BlockSpec(memory_space=pl.ANY),) * 3,
-        scratch_shapes=[dma((3,))],
+        scratch_shapes=[dma((slices + 2,))],
     )(*(pltpu.with_memory_space_constraint(x, pltpu.VMEM) for x in moved))
 
 

time: 41.3 us -> 41.5 us (level)
  no operation moved by 1% of the time
where the time goes in v5:
time: 41.5 us; the launch traced here: 41.3 us
  Pallas kernels  40.7 us (98%)
  between operations  0.64 us (2%)
    pallas_call x1, Pallas kernels, shards(): pl.pallas_call(functools.partial(kernel, n_cuts, n_strip), out_shape=(plt...  39.8 us
    pallas_call x1, Pallas kernels, shards(): pl.pallas_call(hand_out, out_shape=tuple((jax.ShapeDtypeStruct(x.shape, x...  0.84 us

profile of v5, /device:TPU:2, one launch (start us, length us, event | category | flops | bytes accessed | tf_op | source)
XLA Modules:
  0.0 41.3 jit_solution(10801749896732346711)
XLA Ops:
  0.6 39.8 %shard_map.94 = (f32[4,2,32,512]{3,2,1,0:T(8,128)S(1)}, f32[4,1024]{1,0:T(4,128)S(1)}, f32[4,1024]{1,0:T(4,128)S(1)}) custom-call(f32[4,2,32,512]{3,2,1,0:T(8,128)} %field_in.1, f32[4,1024]{1,0:T(4,128)} %phase_in.1, f32[4,1024]{1,0:T(4,128)} %energy_in.1, s32[4,1024]{1,0:T(4,128)} %row_in.1, s32[4,1024]{1,0:T(4,128)} %col_in.1, ...), custom_call_target="tpu_custom_call" | custom-call | tf_op jit(solution)/shard_map/pallas_call | solution.py:354
  40.5 0.8 %shard_map.95 = (f32[4,2,32,512]{3,2,1,0:T(8,128)}, f32[4,1024]{1,0:T(4,128)}, f32[4,1024]{1,0:T(4,128)}) custom-call(f32[4,2,32,512]{3,2,1,0:T(8,128)S(1)} %get-tuple-element.6.field, f32[4,1024]{1,0:T(4,128)S(1)} %get-tuple-element.7.phase, f32[4,1024]{1,0:T(4,128)S(1)} %get-tuple-element.8.energy), custom_call_target="tpu_custom_call" | custom-call | tf_op jit(solution)/shard_map/pallas_call | solution.py:380
